TPU v7x, 32 devices: a whole 2x2x4 slice. The times are simulated.
32 devices in a mesh: clips: 2 (over y), ctx: 4 (over z), head: 4 (over x, core).
Axes of the slice: x: 2, y: 2, z: 4, core: 2. Of those that a mesh axis runs over, the one named last changes fastest.
Arguments:
- queries: bfloat16 [9216, 1536], P(('clips', 'ctx', 'head')), parts along dimension 0
- keys: bfloat16 [9216, 1536], P(('clips', 'ctx', 'head')), parts along dimension 0
- values: bfloat16 [9216, 1536], P(('clips', 'ctx', 'head')), parts along dimension 0, may hold values from -4.5 to 4.5
- neighbors: int32 [24, 8], P(('clips', 'ctx')), parts along dimension 0, may hold values from 0 to 11, as said below
- tile_counts: int32 [24], P(('clips', 'ctx')), parts along dimension 0, may hold values from 192 to 384
Outputs:
- attended: bfloat16 [9216, 1536], P(('clips', 'ctx', 'head')), parts along dimension 0
There are 2 independent parts, one for each index of `clips`. A program takes and returns all parts, laid end to end along the dimension named above; each array names one. Nothing has to cross between parts.
Inputs may be any that keep to these rules, and one draw needn't show every extreme that they name: `neighbors`: row t starts with t itself, followed by 8 - 1 distinct other tiles of t's 3 x 3 x 3 window of tiles: frame layer, row and column each differ from t's by at most one.
All inputs are finite; a program needn't handle non-finite values.
Results may differ from a plain program's by a relative error of at most 0.0049.
Values may be sent and summed in bfloat16 or wider, within the bound.
A program may use at most 64 MiB of HBM per device.

v0:
```python
import jax
import jax.numpy as jnp
from jax import lax
from jax.sharding import PartitionSpec as P

DH = 128
TILE = 384
NB = 8
REACH = 10
HOPS = 4


def shifted(array, axis, by):
    peers = lax.axis_size(axis)
    pairs = [(i, i + by) for i in range(peers) if 0 <= i + by < peers]
    return lax.ppermute(array, axis, pairs)


def join_pieces(pieces):
    return tuple(
        (jnp.concatenate([piece[member] for piece in pieces], axis=0) for member in range(3))
    )


def shards(queries, keys, values, neighbors, tile_counts):
    block_queries, block_keys, block_values = (
        lax.all_to_all(queries, "head", split_axis=1, concat_axis=0, tiled=True),
        lax.all_to_all(keys, "head", split_axis=1, concat_axis=0, tiled=True),
        lax.all_to_all(values, "head", split_axis=1, concat_axis=0, tiled=True),
    )
    tiles_here = tile_counts.shape[0]
    local_width = block_queries.shape[1]
    local_heads = local_width // DH
    earlier = []
    later = []
    for distance in range(1, HOPS + 1):
        taken = min(tiles_here, REACH - (distance - 1) * tiles_here)
        rows_taken = taken * TILE
        sent_back = (block_keys[-rows_taken:], block_values[-rows_taken:], tile_counts[-taken:])
        earlier = [shifted((sent_back[0], sent_back[1], sent_back[2]), "ctx", distance)] + earlier
        sent_fore = (block_keys[:rows_taken], block_values[:rows_taken], tile_counts[:taken])
        later = later + [shifted((sent_fore[0], sent_fore[1], sent_fore[2]), "ctx", -distance)]
    before = join_pieces(earlier)
    after = join_pieces(later)
    ext_tiles = tiles_here + 2 * REACH
    ext_keys = jnp.concatenate([before[0], block_keys, after[0]], axis=0).reshape(
        ext_tiles, TILE, local_width
    )
    ext_values = jnp.concatenate([before[1], block_values, after[1]], axis=0).reshape(
        ext_tiles, TILE, local_width
    )
    ext_counts = jnp.concatenate([before[2], tile_counts, after[2]], axis=0)
    slot_index = jnp.arange(TILE, dtype=jnp.int32)
    key_live = slot_index[None, :] < ext_counts[:, None]
    first_tile = lax.axis_index("ctx") * tiles_here - REACH
    local_lists = jnp.clip(neighbors - first_tile, 0, ext_tiles - 1)
    query_tiles = block_queries.reshape(tiles_here, TILE, local_width)

    def one_tile(tile_index):
        query_block = query_tiles[tile_index]
        listed = local_lists[tile_index]
        key_block = ext_keys[listed].reshape(NB * TILE, local_width)
        value_block = ext_values[listed].reshape(NB * TILE, local_width)
        key_mask = key_live[listed].reshape(NB * TILE)

        def one_head(head_index, result):
            start = head_index * DH
            query_rows = lax.dynamic_slice_in_dim(query_block, start, DH, 1)
            key_rows = lax.dynamic_slice_in_dim(key_block, start, DH, 1)
            value_rows = lax.dynamic_slice_in_dim(value_block, start, DH, 1)
            scores = lax.dot_general(
                query_rows, key_rows, (((1,), (1,)), ((), ())), preferred_element_type=jnp.float32
            ) * DH ** (-0.5)
            scores = jnp.where(key_mask[None, :], scores, -jnp.inf)
            highest = jnp.max(scores, axis=1, keepdims=True)
            weights = jnp.exp(scores - highest)
            totals = jnp.sum(weights, axis=1, keepdims=True)
            rounded = weights.astype(jnp.bfloat16)
            summed = jnp.dot(rounded, value_rows, preferred_element_type=jnp.float32)
            head_out = (summed / totals).astype(jnp.bfloat16)
            return lax.dynamic_update_slice_in_dim(result, head_out, start, 1)

        empty = jnp.zeros((TILE, local_width), jnp.bfloat16)
        return lax.fori_loop(0, local_heads, one_head, empty)

    outputs = lax.map(one_tile, jnp.arange(tiles_here, dtype=jnp.int32))
    outputs = outputs.reshape(tiles_here * TILE, local_width)
    return lax.all_to_all(outputs, "head", split_axis=0, concat_axis=1, tiled=True)


def solution(mesh):
    placed = (
        P(("clips", "ctx", "head"), None),
        P(("clips", "ctx", "head"), None),
        P(("clips", "ctx", "head"), None),
        P(("clips", "ctx"), None),
        P(("clips", "ctx")),
    )
    return jax.shard_map(
        shards,
        mesh=mesh,
        in_specs=placed,
        out_specs=P(("clips", "ctx", "head"), None),
        check_vma=False,
    )
```

profile of v0, /device:TPU:0, one launch (start us, length us, event | category | flops | bytes accessed | tf_op | source)
XLA Modules:
  0.0 357.6 jit_solution(14620852755360953468)
XLA Ops:
  0.0 2.2 copy.22
  2.3 4.2 %all-to-all-start.2 = ((bf16[288,4,384]{2,0,1:T(8,128)(2,1)}), bf16[288,4,384]{2,0,1:T(8,128)(2,1)S(1)}, u32[]{:S(2)}, u32[]{:S(2)}) async-start(bf16[288,4,384]{2,0,1:T(8,128)(2,1)} %bitcast.39), calls=%async_computation.2 | async-start | bytes 1769472 | tf_op jit(solution)/shard_map/all_to_all | solution.py:29
  6.5 2.2 copy.23
  8.7 10.5 %all-to-all-done.2 = bf16[288,4,384]{2,0,1:T(8,128)(2,1)S(1)} async-done(((bf16[288,4,384]{2,0,1:T(8,128)(2,1)}), bf16[288,4,384]{2,0,1:T(8,128)(2,1)S(1)}, u32[]{:S(2)}, u32[]{:S(2)}) %all-to-all-start.2) | async-done | bytes 884768 | tf_op jit(solution)/shard_map/all_to_all | solution.py:29
  19.2 3.5 all-to-all-start.1
  22.7 6.2 %collective-permute-start.17 = (s32[3]{0:T(128)S(1)}, s32[3]{0:T(128)S(1)}, u32[]{:S(2)}, u32[]{:S(2)}) collective-permute-start(s32[3]{0:T(128)S(1)} %copy-done.4), channel_id=1, source_target_pairs={{0,12},{1,13},{2,14},{3,15},{16,28},{17,29},{18,30},{19,31}} | collective-permute-start | bytes 44 | tf_op jit(solution)/shard_map/ppermute | solution.py:16
  29.5 1.2 collective-permute-start.16
  31.8 1.3 collective-permute-start.9
  33.1 1.3 collective-permute-start.10
  35.3 1.4 collective-permute-start.8
  36.7 4.2 %all-to-all-start = ((bf16[288,4,384]{2,0,1:T(8,128)(2,1)}), bf16[288,4,384]{2,0,1:T(8,128)(2,1)}, u32[]{:S(2)}, u32[]{:S(2)}) async-start(bf16[288,4,384]{2,0,1:T(8,128)(2,1)} %bitcast.41), calls=%async_computation | async-start | bytes 1769472 | tf_op jit(solution)/shard_map/all_to_all | solution.py:27
  41.9 1.2 collective-permute-start.23
  43.1 3.8 %collective-permute-start.18 = (s32[3]{0:T(128)S(1)}, s32[3]{0:T(128)S(1)}, u32[]{:S(2)}, u32[]{:S(2)}) collective-permute-start(s32[3]{0:T(128)S(1)} %copy-done.4), channel_id=1, source_target_pairs={{0,8},{4,12},{1,9},{5,13},{2,10},{6,14},{3,11},{7,15},{16,24},{20,... | collective-permute-start | bytes 44 | tf_op jit(solution)/shard_map/ppermute | solution.py:16
  46.9 3.5 collective-permute-start.19
  50.4 21.2 %collective-permute-done.18 = s32[3]{0:T(128)S(1)} collective-permute-done((s32[3]{0:T(128)S(1)}, s32[3]{0:T(128)S(1)}, u32[]{:S(2)}, u32[]{:S(2)}) %collective-permute-start.18) | collective-permute-done | bytes 44 | tf_op jit(solution)/shard_map/ppermute | solution.py:16
  71.6 1.3 collective-permute-start.20
  72.9 1.3 collective-permute-start.21
  74.2 21.3 %collective-permute-done.20 = s32[3]{0:T(128)S(1)} collective-permute-done((s32[3]{0:T(128)S(1)}, s32[3]{0:T(128)S(1)}, u32[]{:S(2)}, u32[]{:S(2)}) %collective-permute-start.20) | collective-permute-done | bytes 44 | tf_op jit(solution)/shard_map/ppermute | solution.py:16
  95.5 1.3 collective-permute-start.22
  96.8 1.5 collective-permute-done.21
  98.2 4.9 %collective-permute-start.11 = (bf16[1152,384]{1,0:T(8,128)(2,1)S(1)}, bf16[1152,384]{1,0:T(8,128)(2,1)}, u32[]{:S(2)}, u32[]{:S(2)}) collective-permute-start(bf16[1152,384]{1,0:T(8,128)(2,1)S(1)} %bitcast.69), channel_id=1, source_target_pairs={{0,4},{4,8},{8,12},{1,5},{5,9},{9,13},{2,6},{6,10},{10,14},{3,7},{... | collective-permute-start | bytes 2654216 | tf_op jit(solution)/shard_map/ppermute | solution.py:16
  103.7 1.4 collective-permute-start
  105.1 2.1 concatenate.11
  107.1 1.3 collective-permute-start.12
  108.4 1.7 constant_dynamic-update-slice_fusion.17
  110.1 1.3 collective-permute-start.13
  111.4 1.7 constant_dynamic-update-slice_fusion.8
  113.1 7.6 %collective-permute-start.1 = (bf16[1152,384]{1,0:T(8,128)(2,1)S(1)}, bf16[1152,384]{1,0:T(8,128)(2,1)S(1)}, u32[]{:S(2)}, u32[]{:S(2)}) collective-permute-start(bf16[1152,384]{1,0:T(8,128)(2,1)S(1)} %bitcast.59), channel_id=1, source_target_pairs={{0,12},{1,13},{2,14},{3,15},{16,28},{17,29},{18,30},{19,31}} | collective-permute-start | bytes 2654216 | tf_op jit(solution)/shard_map/ppermute | solution.py:16
  120.7 1.1 constant_dynamic-update-slice_fusion.16
  121.8 1.5 collective-permute-start.2
  123.3 1.1 constant_dynamic-update-slice_fusion.15
  124.4 2.6 collective-permute-start.3
  127.0 2.2 constant_dynamic-update-slice_fusion.14
  130.1 10.6 %collective-permute-done.1 = bf16[1152,384]{1,0:T(8,128)(2,1)S(1)} collective-permute-done((bf16[1152,384]{1,0:T(8,128)(2,1)S(1)}, bf16[1152,384]{1,0:T(8,128)(2,1)S(1)}, u32[]{:S(2)}, u32[]{:S(2)}) %collective-permute-start.1) | collective-permute-done | bytes 884768 | tf_op jit(solution)/shard_map/ppermute | solution.py:16
  140.8 1.3 collective-permute-start.14
  143.1 16.6 %collective-permute-done.2 = bf16[1152,384]{1,0:T(8,128)(2,1)S(1)} collective-permute-done((bf16[1152,384]{1,0:T(8,128)(2,1)S(1)}, bf16[1152,384]{1,0:T(8,128)(2,1)S(1)}, u32[]{:S(2)}, u32[]{:S(2)}) %collective-permute-start.2) | collective-permute-done | bytes 884768 | tf_op jit(solution)/shard_map/ppermute | solution.py:16
  159.7 1.3 collective-permute-start.4
  162.0 15.1 %collective-permute-done.3 = bf16[1152,384]{1,0:T(8,128)(2,1)S(1)} collective-permute-done((bf16[1152,384]{1,0:T(8,128)(2,1)S(1)}, bf16[1152,384]{1,0:T(8,128)(2,1)S(1)}, u32[]{:S(2)}, u32[]{:S(2)}) %collective-permute-start.3) | collective-permute-done | bytes 884768 | tf_op jit(solution)/shard_map/ppermute | solution.py:16
  177.1 1.3 collective-permute-start.5
  180.4 1.3 collective-permute-start.6
  182.7 4.3 %collective-permute-done.13 = bf16[1152,384]{1,0:T(8,128)(2,1)S(1)} collective-permute-done((bf16[1152,384]{1,0:T(8,128)(2,1)S(1)}, bf16[1152,384]{1,0:T(8,128)(2,1)S(1)}, u32[]{:S(2)}, u32[]{:S(2)}) %collective-permute-start.13) | collective-permute-done | bytes 884768 | tf_op jit(solution)/shard_map/ppermute | solution.py:16
  190.4 13.4 %collective-permute-done.4 = bf16[1152,384]{1,0:T(8,128)(2,1)S(1)} collective-permute-done((bf16[1152,384]{1,0:T(8,128)(2,1)S(1)}, bf16[1152,384]{1,0:T(8,128)(2,1)S(1)}, u32[]{:S(2)}, u32[]{:S(2)}) %collective-permute-start.4) | collective-permute-done | bytes 884768 | tf_op jit(solution)/shard_map/ppermute | solution.py:16
  204.8 55.9 %collective-permute-done.5 = bf16[1152,384]{1,0:T(8,128)(2,1)S(1)} collective-permute-done((bf16[1152,384]{1,0:T(8,128)(2,1)S(1)}, bf16[1152,384]{1,0:T(8,128)(2,1)S(1)}, u32[]{:S(2)}, u32[]{:S(2)}) %collective-permute-start.5) | collective-permute-done | bytes 884768 | tf_op jit(solution)/shard_map/ppermute | solution.py:16
  260.7 1.1 constant_dynamic-update-slice_fusion.2
  264.3 76.2 %while.27 = (s32[]{:T(128)}, bf16[3,384,384]{2,1,0:T(8,128)(2,1)}, s32[3]{0:T(128)S(1)}, bf16[3,384,384]{2,1,0:T(8,128)(2,1)}, s32[3,8]{1,0:T(4,128)S(1)}, /*ind...) while((s32[]{:T(128)}, bf16[3,384,384]{2,1,0:T(8,128)(2,1)}, ...), condition=%wide.region_5.6_spmd.clone, body=%wide.region_0.5_spmd.clone.sunk | while | flops 612344704 | bytes 26889600 | solution.py:86
  267.5 4.0 %gather_fusion.1 = bf16[8,384,384]{2,1,0:T(8,128)(2,1)S(1)} fusion(bf16[23,384,384]{2,1,0:T(8,128)(2,1)} %get-tuple-element.422, s32[1024]{0:T(1024)S(1)} %pad_clamp_fusion.2), kind=kCustom, calls=%fused_computation.1.clone.clone.1 | custom fusion | bytes 4718624 | tf_op jit(solution)/shard_map/while/body/eval_jaxpr/gather | solution.py:62
  271.5 5.2 %gather_fusion.2 = bf16[8,384,384]{2,1,0:T(8,128)(2,1)} fusion(bf16[23,384,384]{2,1,0:T(8,128)(2,1)} %get-tuple-element.423, s32[1024]{0:T(1024)S(1)} %pad_clamp_fusion.2), kind=kCustom, calls=%fused_computation.2.clone.clone.1 | custom fusion | bytes 4718624 | tf_op jit(solution)/shard_map/while/body/eval_jaxpr/gather | solution.py:63
  277.7 11.2 %while.28 = (s32[]{:T(128)}, bf16[384,384]{1,0:T(8,128)(2,1)S(1)}, pred[8,384]{1,0:T(8,128)(4,1)}, bf16[384,384]{1,0:T(8,128)(2,1)S(1)}, bf16[3072,384]{1,0:T(8,...) while((s32[]{:T(128)}, bf16[384,384]{1,0:T(8,128)(2,1)S(1)}, ...), condition=%wide.wide.region_4.4_spmd, body=%wide.wide.region_1.3_spmd.sunk | while | flops 612334848 | bytes 15939227 | solution.py:84
  279.4 2.0 fusion.43
  283.2 2.0 fusion.43
  286.9 2.0 fusion.43
  292.9 4.0 %gather_fusion.1 = bf16[8,384,384]{2,1,0:T(8,128)(2,1)S(1)} fusion(bf16[23,384,384]{2,1,0:T(8,128)(2,1)} %get-tuple-element.422, s32[1024]{0:T(1024)S(1)} %pad_clamp_fusion.2), kind=kCustom, calls=%fused_computation.1.clone.clone.1 | custom fusion | bytes 4718624 | tf_op jit(solution)/shard_map/while/body/eval_jaxpr/gather | solution.py:62
  296.8 5.2 %gather_fusion.2 = bf16[8,384,384]{2,1,0:T(8,128)(2,1)} fusion(bf16[23,384,384]{2,1,0:T(8,128)(2,1)} %get-tuple-element.423, s32[1024]{0:T(1024)S(1)} %pad_clamp_fusion.2), kind=kCustom, calls=%fused_computation.2.clone.clone.1 | custom fusion | bytes 4718624 | tf_op jit(solution)/shard_map/while/body/eval_jaxpr/gather | solution.py:63
  303.1 11.2 %while.28 = (s32[]{:T(128)}, bf16[384,384]{1,0:T(8,128)(2,1)S(1)}, pred[8,384]{1,0:T(8,128)(4,1)}, bf16[384,384]{1,0:T(8,128)(2,1)S(1)}, bf16[3072,384]{1,0:T(8,...) while((s32[]{:T(128)}, bf16[384,384]{1,0:T(8,128)(2,1)S(1)}, ...), condition=%wide.wide.region_4.4_spmd, body=%wide.wide.region_1.3_spmd.sunk | while | flops 612334848 | bytes 15939227 | solution.py:84
  304.8 2.0 fusion.43
  308.5 2.0 fusion.43
  312.3 2.0 fusion.43
  318.2 4.0 %gather_fusion.1 = bf16[8,384,384]{2,1,0:T(8,128)(2,1)S(1)} fusion(bf16[23,384,384]{2,1,0:T(8,128)(2,1)} %get-tuple-element.422, s32[1024]{0:T(1024)S(1)} %pad_clamp_fusion.2), kind=kCustom, calls=%fused_computation.1.clone.clone.1 | custom fusion | bytes 4718624 | tf_op jit(solution)/shard_map/while/body/eval_jaxpr/gather | solution.py:62
  322.2 5.2 %gather_fusion.2 = bf16[8,384,384]{2,1,0:T(8,128)(2,1)} fusion(bf16[23,384,384]{2,1,0:T(8,128)(2,1)} %get-tuple-element.423, s32[1024]{0:T(1024)S(1)} %pad_clamp_fusion.2), kind=kCustom, calls=%fused_computation.2.clone.clone.1 | custom fusion | bytes 4718624 | tf_op jit(solution)/shard_map/while/body/eval_jaxpr/gather | solution.py:63
  328.5 11.2 %while.28 = (s32[]{:T(128)}, bf16[384,384]{1,0:T(8,128)(2,1)S(1)}, pred[8,384]{1,0:T(8,128)(4,1)}, bf16[384,384]{1,0:T(8,128)(2,1)S(1)}, bf16[3072,384]{1,0:T(8,...) while((s32[]{:T(128)}, bf16[384,384]{1,0:T(8,128)(2,1)S(1)}, ...), condition=%wide.wide.region_4.4_spmd, body=%wide.wide.region_1.3_spmd.sunk | while | flops 612334848 | bytes 15939227 | solution.py:84
  330.2 2.0 fusion.43
  333.9 2.0 fusion.43
  337.7 2.0 fusion.43
  340.5 16.1 %all_to_all.73 = bf16[4,288,384]{2,1,0:T(8,128)(2,1)S(1)} all-to-all(bf16[4,288,384]{2,1,0:T(8,128)(2,1)} %bitcast.78), channel_id=1, replica_groups=mesh['clips'=2,'ctx'=4,'head'=4] {'head'}, dimensions={0} | all-to-all | bytes 1769472 | tf_op jit(solution)/shard_map/all_to_all | solution.py:88
  (110 shorter events, 42.3 us)
Async XLA Ops:
  0.0 22.7 %copy-start.4 = (s32[3]{0:T(128)S(1)}, s32[3]{0:T(128)}, u32[]{:S(2)}) copy-start(s32[3]{0:T(128)} %param.13) | copy-start | bytes 40
  0.0 30.7 %copy-start = (bf16[288,1536]{1,0:T(8,128)(2,1)S(1)}, bf16[288,1536]{1,0:T(8,128)(2,1)}, u32[]{:S(2)}) copy-start(bf16[288,1536]{1,0:T(8,128)(2,1)} %param.9) | copy-start | bytes 2654212
  0.0 105.1 %copy-start.5 = (s32[3,8]{1,0:T(4,128)S(1)}, s32[3,8]{1,0:T(4,128)}, u32[]{:S(2)}) copy-start(s32[3,8]{1,0:T(4,128)} %param.12) | copy-start | bytes 292
  2.3 16.9 %all-to-all-start.2 = ((bf16[288,4,384]{2,0,1:T(8,128)(2,1)}), bf16[288,4,384]{2,0,1:T(8,128)(2,1)S(1)}, u32[]{:S(2)}, u32[]{:S(2)}) async-start(bf16[288,4,384]{2,0,1:T(8,128)(2,1)} %bitcast.39), calls=%async_computation.2 | async-start | bytes 1769472 | tf_op jit(solution)/shard_map/all_to_all | solution.py:29
  19.2 17.5 %all-to-all-start.1 = ((bf16[288,4,384]{2,0,1:T(8,128)(2,1)}), bf16[288,4,384]{2,0,1:T(8,128)(2,1)S(1)}, u32[]{:S(2)}, u32[]{:S(2)}) async-start(bf16[288,4,384]{2,0,1:T(8,128)(2,1)} %bitcast.40), calls=%async_computation.1 | async-start | bytes 1769472 | tf_op jit(solution)/shard_map/all_to_all | solution.py:28
  22.7 24.2 %collective-permute-start.17 = (s32[3]{0:T(128)S(1)}, s32[3]{0:T(128)S(1)}, u32[]{:S(2)}, u32[]{:S(2)}) collective-permute-start(s32[3]{0:T(128)S(1)} %copy-done.4), channel_id=1, source_target_pairs={{0,12},{1,13},{2,14},{3,15},{16,28},{17,29},{18,30},{19,31}} | collective-permute-start | bytes 44 | tf_op jit(solution)/shard_map/ppermute | solution.py:16
  29.5 12.3 %collective-permute-start.16 = (s32[1]{0:T(128)}, s32[1]{0:T(128)}, u32[]{:S(2)}, u32[]{:S(2)}) collective-permute-start(s32[1]{0:T(128)} %get-tuple-element.212), channel_id=1, source_target_pairs={} | collective-permute-start | bytes 20 | tf_op jit(solution)/shard_map/ppermute | solution.py:16
  31.8 81.4 %collective-permute-start.9 = (bf16[1152,384]{1,0:T(8,128)(2,1)S(1)}, bf16[1152,384]{1,0:T(8,128)(2,1)S(1)}, u32[]{:S(2)}, u32[]{:S(2)}) collective-permute-start(bf16[1152,384]{1,0:T(8,128)(2,1)S(1)} %bitcast.66), channel_id=1, source_target_pairs={{0,12},{1,13},{2,14},{3,15},{16,28},{17,29},{18,30},{19,31}} | collective-permute-start | bytes 2654216 | tf_op jit(solution)/shard_map/ppermute | solution.py:16
  33.1 88.7 %collective-permute-start.10 = (bf16[1152,384]{1,0:T(8,128)(2,1)S(1)}, bf16[1152,384]{1,0:T(8,128)(2,1)S(1)}, u32[]{:S(2)}, u32[]{:S(2)}) collective-permute-start(bf16[1152,384]{1,0:T(8,128)(2,1)S(1)} %bitcast.67), channel_id=1, source_target_pairs={{0,8},{4,12},{1,9},{5,13},{2,10},{6,14},{3,11},{7,15},{16,24},{20,... | collective-permute-start | bytes 2654216 | tf_op jit(solution)/shard_map/ppermute | solution.py:16
  35.3 71.8 %collective-permute-start.8 = (bf16[384,384]{1,0:T(8,128)(2,1)}, bf16[384,384]{1,0:T(8,128)(2,1)}, u32[]{:S(2)}, u32[]{:S(2)}) collective-permute-start(bf16[384,384]{1,0:T(8,128)(2,1)} %get-tuple-element.208), channel_id=1, source_target_pairs={} | collective-permute-start | bytes 884744 | tf_op jit(solution)/shard_map/ppermute | solution.py:16
  36.7 227.6 %all-to-all-start = ((bf16[288,4,384]{2,0,1:T(8,128)(2,1)}), bf16[288,4,384]{2,0,1:T(8,128)(2,1)}, u32[]{:S(2)}, u32[]{:S(2)}) async-start(bf16[288,4,384]{2,0,1:T(8,128)(2,1)} %bitcast.41), calls=%async_computation | async-start | bytes 1769472 | tf_op jit(solution)/shard_map/all_to_all | solution.py:27
  41.9 1.2 collective-permute-start.23
  43.1 28.5 %collective-permute-start.18 = (s32[3]{0:T(128)S(1)}, s32[3]{0:T(128)S(1)}, u32[]{:S(2)}, u32[]{:S(2)}) collective-permute-start(s32[3]{0:T(128)S(1)} %copy-done.4), channel_id=1, source_target_pairs={{0,8},{4,12},{1,9},{5,13},{2,10},{6,14},{3,11},{7,15},{16,24},{20,... | collective-permute-start | bytes 44 | tf_op jit(solution)/shard_map/ppermute | solution.py:16
  46.9 26.0 %collective-permute-start.19 = (s32[3]{0:T(128)S(1)}, s32[3]{0:T(128)S(1)}, u32[]{:S(2)}, u32[]{:S(2)}) collective-permute-start(s32[3]{0:T(128)S(1)} %copy-done.4), channel_id=1, source_target_pairs={{0,4},{4,8},{8,12},{1,5},{5,9},{9,13},{2,6},{6,10},{10,14},{3,7},{... | collective-permute-start | bytes 44 | tf_op jit(solution)/shard_map/ppermute | solution.py:16
  71.6 31.6 %copy-start.6 = (s32[3]{0:T(128)}, s32[3]{0:T(128)S(1)}, u32[]{:S(2)}) copy-start(s32[3]{0:T(128)S(1)} %collective-permute-done.18) | copy-start | bytes 40
  71.6 23.9 %collective-permute-start.20 = (s32[3]{0:T(128)S(1)}, s32[3]{0:T(128)S(1)}, u32[]{:S(2)}, u32[]{:S(2)}) collective-permute-start(s32[3]{0:T(128)S(1)} %copy-done.4), channel_id=1, source_target_pairs={{4,0},{8,4},{12,8},{5,1},{9,5},{13,9},{6,2},{10,6},{14,10},{7,3},{... | collective-permute-start | bytes 44 | tf_op jit(solution)/shard_map/ppermute | solution.py:16
  72.9 30.3 %copy-start.7 = (s32[3]{0:T(128)}, s32[3]{0:T(128)S(1)}, u32[]{:S(2)}) copy-start(s32[3]{0:T(128)S(1)} %collective-permute-done.19) | copy-start | bytes 40
  72.9 25.3 %collective-permute-start.21 = (s32[3]{0:T(128)S(1)}, s32[3]{0:T(128)S(1)}, u32[]{:S(2)}, u32[]{:S(2)}) collective-permute-start(s32[3]{0:T(128)S(1)} %copy-done.4), channel_id=1, source_target_pairs={{8,0},{12,4},{9,1},{13,5},{10,2},{14,6},{11,3},{15,7},{24,16},{28,... | collective-permute-start | bytes 44 | tf_op jit(solution)/shard_map/ppermute | solution.py:16
  95.5 7.7 %copy-start.8 = (s32[3]{0:T(128)}, s32[3]{0:T(128)S(1)}, u32[]{:S(2)}) copy-start(s32[3]{0:T(128)S(1)} %collective-permute-done.20) | copy-start | bytes 40
  95.5 7.7 %collective-permute-start.22 = (s32[3]{0:T(128)S(1)}, s32[3]{0:T(128)S(1)}, u32[]{:S(2)}, u32[]{:S(2)}) collective-permute-start(s32[3]{0:T(128)S(1)} %copy-done.4), channel_id=1, source_target_pairs={{12,0},{13,1},{14,2},{15,3},{28,16},{29,17},{30,18},{31,19}} | collective-permute-start | bytes 44 | tf_op jit(solution)/shard_map/ppermute | solution.py:16
  98.2 5.0 %copy-start.9 = (s32[3]{0:T(128)}, s32[3]{0:T(128)S(1)}, u32[]{:S(2)}) copy-start(s32[3]{0:T(128)S(1)} %collective-permute-done.21) | copy-start | bytes 40
  98.2 26.1 %collective-permute-start.11 = (bf16[1152,384]{1,0:T(8,128)(2,1)S(1)}, bf16[1152,384]{1,0:T(8,128)(2,1)}, u32[]{:S(2)}, u32[]{:S(2)}) collective-permute-start(bf16[1152,384]{1,0:T(8,128)(2,1)S(1)} %bitcast.69), channel_id=1, source_target_pairs={{0,4},{4,8},{8,12},{1,5},{5,9},{9,13},{2,6},{6,10},{10,14},{3,7},{... | collective-permute-start | bytes 2654216 | tf_op jit(solution)/shard_map/ppermute | solution.py:16
  103.2 0.5 copy-start.10
  103.7 6.4 %collective-permute-start = (bf16[384,384]{1,0:T(8,128)(2,1)}, bf16[384,384]{1,0:T(8,128)(2,1)}, u32[]{:S(2)}, u32[]{:S(2)}) collective-permute-start(bf16[384,384]{1,0:T(8,128)(2,1)} %get-tuple-element.210), channel_id=1, source_target_pairs={} | collective-permute-start | bytes 884744 | tf_op jit(solution)/shard_map/ppermute | solution.py:16
  107.1 73.3 %collective-permute-start.12 = (bf16[1152,384]{1,0:T(8,128)(2,1)S(1)}, bf16[1152,384]{1,0:T(8,128)(2,1)S(1)}, u32[]{:S(2)}, u32[]{:S(2)}) collective-permute-start(bf16[1152,384]{1,0:T(8,128)(2,1)S(1)} %bitcast.70), channel_id=1, source_target_pairs={{4,0},{8,4},{12,8},{5,1},{9,5},{13,9},{6,2},{10,6},{14,10},{7,3},{... | collective-permute-start | bytes 2654216 | tf_op jit(solution)/shard_map/ppermute | solution.py:16
  110.1 76.9 %collective-permute-start.13 = (bf16[1152,384]{1,0:T(8,128)(2,1)S(1)}, bf16[1152,384]{1,0:T(8,128)(2,1)S(1)}, u32[]{:S(2)}, u32[]{:S(2)}) collective-permute-start(bf16[1152,384]{1,0:T(8,128)(2,1)S(1)} %bitcast.71), channel_id=1, source_target_pairs={{8,0},{12,4},{9,1},{13,5},{10,2},{14,6},{11,3},{15,7},{24,16},{28,... | collective-permute-start | bytes 2654216 | tf_op jit(solution)/shard_map/ppermute | solution.py:16
  113.1 27.6 %collective-permute-start.1 = (bf16[1152,384]{1,0:T(8,128)(2,1)S(1)}, bf16[1152,384]{1,0:T(8,128)(2,1)S(1)}, u32[]{:S(2)}, u32[]{:S(2)}) collective-permute-start(bf16[1152,384]{1,0:T(8,128)(2,1)S(1)} %bitcast.59), channel_id=1, source_target_pairs={{0,12},{1,13},{2,14},{3,15},{16,28},{17,29},{18,30},{19,31}} | collective-permute-start | bytes 2654216 | tf_op jit(solution)/shard_map/ppermute | solution.py:16
  121.8 65.2 %copy-start.2 = (bf16[384,384]{1,0:T(8,128)(2,1)S(1)}, bf16[384,384]{1,0:T(8,128)(2,1)}, u32[]{:S(2)}) copy-start(bf16[384,384]{1,0:T(8,128)(2,1)} %get-tuple-element.207) | copy-start | bytes 884740
  121.8 37.9 %collective-permute-start.2 = (bf16[1152,384]{1,0:T(8,128)(2,1)S(1)}, bf16[1152,384]{1,0:T(8,128)(2,1)S(1)}, u32[]{:S(2)}, u32[]{:S(2)}) collective-permute-start(bf16[1152,384]{1,0:T(8,128)(2,1)S(1)} %bitcast.60), channel_id=1, source_target_pairs={{0,8},{4,12},{1,9},{5,13},{2,10},{6,14},{3,11},{7,15},{16,24},{20,... | collective-permute-start | bytes 2654216 | tf_op jit(solution)/shard_map/ppermute | solution.py:16
  124.4 64.3 %copy-start.3 = (bf16[384,384]{1,0:T(8,128)(2,1)S(1)}, bf16[384,384]{1,0:T(8,128)(2,1)}, u32[]{:S(2)}) copy-start(bf16[384,384]{1,0:T(8,128)(2,1)} %get-tuple-element.209) | copy-start | bytes 884740
  124.4 52.7 %collective-permute-start.3 = (bf16[1152,384]{1,0:T(8,128)(2,1)S(1)}, bf16[1152,384]{1,0:T(8,128)(2,1)S(1)}, u32[]{:S(2)}, u32[]{:S(2)}) collective-permute-start(bf16[1152,384]{1,0:T(8,128)(2,1)S(1)} %bitcast.61), channel_id=1, source_target_pairs={{0,4},{4,8},{8,12},{1,5},{5,9},{9,13},{2,6},{6,10},{10,14},{3,7},{... | collective-permute-start | bytes 2654216 | tf_op jit(solution)/shard_map/ppermute | solution.py:16
  140.8 47.9 %collective-permute-start.14 = (bf16[1152,384]{1,0:T(8,128)(2,1)S(1)}, bf16[1152,384]{1,0:T(8,128)(2,1)S(1)}, u32[]{:S(2)}, u32[]{:S(2)}) collective-permute-start(bf16[1152,384]{1,0:T(8,128)(2,1)S(1)} %bitcast.73), channel_id=1, source_target_pairs={{12,0},{13,1},{14,2},{15,3},{28,16},{29,17},{30,18},{31,19}} | collective-permute-start | bytes 2654216 | tf_op jit(solution)/shard_map/ppermute | solution.py:16
  159.7 44.1 %collective-permute-start.4 = (bf16[1152,384]{1,0:T(8,128)(2,1)S(1)}, bf16[1152,384]{1,0:T(8,128)(2,1)S(1)}, u32[]{:S(2)}, u32[]{:S(2)}) collective-permute-start(bf16[1152,384]{1,0:T(8,128)(2,1)S(1)} %bitcast.62), channel_id=1, source_target_pairs={{4,0},{8,4},{12,8},{5,1},{9,5},{13,9},{6,2},{10,6},{14,10},{7,3},{... | collective-permute-start | bytes 2654216 | tf_op jit(solution)/shard_map/ppermute | solution.py:16
  177.1 83.6 %collective-permute-start.5 = (bf16[1152,384]{1,0:T(8,128)(2,1)S(1)}, bf16[1152,384]{1,0:T(8,128)(2,1)S(1)}, u32[]{:S(2)}, u32[]{:S(2)}) collective-permute-start(bf16[1152,384]{1,0:T(8,128)(2,1)S(1)} %bitcast.63), channel_id=1, source_target_pairs={{8,0},{12,4},{9,1},{13,5},{10,2},{14,6},{11,3},{15,7},{24,16},{28,... | collective-permute-start | bytes 2654216 | tf_op jit(solution)/shard_map/ppermute | solution.py:16
  180.4 82.1 %collective-permute-start.6 = (bf16[1152,384]{1,0:T(8,128)(2,1)S(1)}, bf16[1152,384]{1,0:T(8,128)(2,1)S(1)}, u32[]{:S(2)}, u32[]{:S(2)}) collective-permute-start(bf16[1152,384]{1,0:T(8,128)(2,1)S(1)} %bitcast.65), channel_id=1, source_target_pairs={{12,0},{13,1},{14,2},{15,3},{28,16},{29,17},{30,18},{31,19}} | collective-permute-start | bytes 2654216 | tf_op jit(solution)/shard_map/ppermute | solution.py:16
  187.0 74.8 %collective-permute-start.15 = (bf16[384,384]{1,0:T(8,128)(2,1)S(1)}, bf16[384,384]{1,0:T(8,128)(2,1)S(1)}, u32[]{:S(2)}, u32[]{:S(2)}) collective-permute-start(bf16[384,384]{1,0:T(8,128)(2,1)S(1)} %copy-done.2), channel_id=1, source_target_pairs={} | collective-permute-start | bytes 884744 | tf_op jit(solution)/shard_map/ppermute | solution.py:16
  188.7 74.9 %collective-permute-start.7 = (bf16[384,384]{1,0:T(8,128)(2,1)S(1)}, bf16[384,384]{1,0:T(8,128)(2,1)S(1)}, u32[]{:S(2)}, u32[]{:S(2)}) collective-permute-start(bf16[384,384]{1,0:T(8,128)(2,1)S(1)} %copy-done.3), channel_id=1, source_target_pairs={} | collective-permute-start | bytes 884744 | tf_op jit(solution)/shard_map/ppermute | solution.py:16
  267.4 10.3 %copy-start.1 = (pred[8,384]{1,0:T(8,128)(4,1)}, pred[8,384]{1,0:T(8,128)(4,1)S(1)}, u32[]{:S(2)}) copy-start(pred[8,384]{1,0:T(8,128)(4,1)S(1)} %gather_fusion) | copy-start | bytes 9220 | tf_op jit(solution)/shard_map/while
  292.8 10.3 %copy-start.1 = (pred[8,384]{1,0:T(8,128)(4,1)}, pred[8,384]{1,0:T(8,128)(4,1)S(1)}, u32[]{:S(2)}) copy-start(pred[8,384]{1,0:T(8,128)(4,1)S(1)} %gather_fusion) | copy-start | bytes 9220 | tf_op jit(solution)/shard_map/while
  318.2 10.3 %copy-start.1 = (pred[8,384]{1,0:T(8,128)(4,1)}, pred[8,384]{1,0:T(8,128)(4,1)S(1)}, u32[]{:S(2)}) copy-start(pred[8,384]{1,0:T(8,128)(4,1)S(1)} %gather_fusion) | copy-start | bytes 9220 | tf_op jit(solution)/shard_map/while
where the time goes:
time: 359 us; the launch traced here: 358 us
  waiting for transfers between devices  170 us (47%)
  local copies, waits for them, and re-layouts  68.2 us (19%)
  starting transfers between devices  62.8 us (17%)
  matrix products  26.5 us (7%)
  blocking collectives  16.1 us (4%)
  other arithmetic  7.3 us (2%)
  loops' own time  5.99 us (2%)
    ppermute x24, waiting for transfers between devices, shifted(): return lax.ppermute(array, axis, pairs)  160 us
    ppermute x24, starting transfers between devices, shifted(): return lax.ppermute(array, axis, pairs)  50.8 us
    unnamed x36, local copies, waits for them, and re-layouts  19.4 us
    dot_general x9, matrix products, one_head(): summed = jnp.dot(rounded, value_rows, preferred_element_type=jnp.float32)  18.2 us
    all_to_all x1, blocking collectives, shards(): lax.all_to_all(outputs, 'head', split_axis=0, concat_axis=1, tiled=True)  16.1 us
    gather x3, local copies, waits for them, and re-layouts, one_tile(): value_block = ext_values[listed].reshape(NB * TILE, local_width)  15.6 us
    gather x3, local copies, waits for them, and re-layouts, one_tile(): key_block = ext_keys[listed].reshape(NB * TILE, local_width)  12 us
    all_to_all x1, waiting for transfers between devices, shards(): lax.all_to_all(values, 'head', split_axis=1, concat_axis=0, tiled=True)  10.5 us
  transfers between devices with their start and end apart: 27, of which 10 were waited for; matrix products, arithmetic and copies ran while one was open for 8% of the time, Pallas kernels for 0%

commit v1 on v0

--- a/solution.py
+++ b/solution.py
@@ -8,6 +8,30 @@
 NB = 8
 REACH = 10
 HOPS = 4
+
+
+def sites_obtain(u_in):
+    device_axis = "head"
+    arr_next = lax.axis_size(device_axis)
+    field_out = lax.axis_index(device_axis)
+    x_now, main = (arr_next, field_out)
+    low = u_in.shape[1] // x_now
+    e_now = list(u_in.shape)
+    e_now[1] = low
+    all_rows = e_now[0]
+    e_now[0] = all_rows * x_now
+    long_array = jnp.zeros(e_now, u_in.dtype)
+    for num in range(x_now):
+        q_next = lax.dynamic_slice_in_dim(u_in, (main ^ num) * low, low, axis=1)
+        if num:
+            vals = []
+            for h in range(x_now):
+                vals.append((h, h ^ num))
+            q_next = lax.ppermute(q_next, device_axis, vals)
+        long_array = lax.dynamic_update_slice_in_dim(
+            long_array, q_next, (main ^ num) * all_rows, axis=0
+        )
+    return long_array
 
 
 def shifted(array, axis, by):
@@ -26,7 +50,7 @@
     block_queries, block_keys, block_values = (
         lax.all_to_all(queries, "head", split_axis=1, concat_axis=0, tiled=True),
         lax.all_to_all(keys, "head", split_axis=1, concat_axis=0, tiled=True),
-        lax.all_to_all(values, "head", split_axis=1, concat_axis=0, tiled=True),
+        sites_obtain(values),
     )
     tiles_here = tile_counts.shape[0]
     local_width = block_queries.shape[1]

time: 359 us -> 353 us (0.983)
  waiting for transfers between devices: 170 us -> 131 us
  starting transfers between devices: 62.8 us -> 94.6 us
    ppermute x24, starting transfers between devices: 50.8 us -> 83.6 us  [shifted(): return lax.ppermute(array, axis, pairs)]
    ppermute x24, waiting for transfers between devices: 160 us -> 131 us  [shifted(): return lax.ppermute(array, axis, pairs)]
    all_to_all x1 -> x0, waiting for transfers between devices: 10.5 us -> none  [shards(): lax.all_to_all(values, 'head', split_axis=1, concat_axis=0, tiled=True)]
    all_to_all x1 -> x0, starting transfers between devices: 4.24 us -> none  [shards(): lax.all_to_all(values, 'head', split_axis=1, concat_axis=0, tiled=True)]
    unnamed x36 -> x34, local copies, waits for them, and re-layouts: 19.4 us -> 19.5 us
  transfers between devices with their start and end apart: 27 -> 29, of which waited for: 10 -> 9; matrix products, arithmetic and copies ran while one was open for 8% -> 9% of each run, Pallas kernels for 0% -> 0%
where the time goes in v1:
time: 353 us; the launch traced here: 351 us
  waiting for transfers between devices  131 us (37%)
  starting transfers between devices  94.6 us (27%)
  local copies, waits for them, and re-layouts  70.1 us (20%)
  matrix products  26.5 us (8%)
  blocking collectives  16.1 us (5%)
  other arithmetic  7.3 us (2%)
  loops' own time  5.92 us (2%)
    ppermute x24, waiting for transfers between devices, shifted(): return lax.ppermute(array, axis, pairs)  131 us
    ppermute x24, starting transfers between devices, shifted(): return lax.ppermute(array, axis, pairs)  83.6 us
    unnamed x34, local copies, waits for them, and re-layouts  19.5 us
    dot_general x9, matrix products, one_head(): summed = jnp.dot(rounded, value_rows, preferred_element_type=jnp.float32)  18.3 us
    all_to_all x1, blocking collectives, shards(): lax.all_to_all(outputs, 'head', split_axis=0, concat_axis=1, tiled=True)  16.1 us
    gather x3, local copies, waits for them, and re-layouts, one_tile(): value_block = ext_values[listed].reshape(NB * TILE, local_width)  15.6 us
    gather x3, local copies, waits for them, and re-layouts, one_tile(): key_block = ext_keys[listed].reshape(NB * TILE, local_width)  12 us
    dot_general x9, matrix products, one_head(): lax.dot_general(query_rows, key_rows, (((1,), (1,)), ((), ())), preferred...  8.23 us
  transfers between devices with their start and end apart: 29, of which 9 were waited for; matrix products, arithmetic and copies ran while one was open for 9% of the time, Pallas kernels for 0%

profile of v1, /device:TPU:0, one launch (start us, length us, event | category | flops | bytes accessed | tf_op | source)
XLA Modules:
  0.0 351.4 jit_solution(7729267410968066943)
XLA Ops:
  0.1 1.5 constant_dynamic-slice_fusion.1
  2.1 2.6 collective-permute-start.9
  4.7 2.2 copy.18
  6.9 3.5 all-to-all-start.1
  10.4 5.8 %collective-permute-start.20 = (s32[3]{0:T(128)}, s32[3]{0:T(128)S(1)}, u32[]{:S(2)}, u32[]{:S(2)}) collective-permute-start(s32[3]{0:T(128)} %param.13), channel_id=1, source_target_pairs={{0,12},{1,13},{2,14},{3,15},{16,28},{17,29},{18,30},{19,31}} | collective-permute-start | bytes 44 | tf_op jit(solution)/shard_map/ppermute | solution.py:40
  16.2 1.3 fusion.26
  17.5 1.2 collective-permute-start.19
  21.7 1.4 collective-permute-start.12
  23.1 1.3 collective-permute-start.13
  25.3 1.4 collective-permute-start.11
  26.6 4.2 %all-to-all-start = ((bf16[288,4,384]{2,0,1:T(8,128)(2,1)}), bf16[288,4,384]{2,0,1:T(8,128)(2,1)}, u32[]{:S(2)}, u32[]{:S(2)}) async-start(bf16[288,4,384]{2,0,1:T(8,128)(2,1)} %bitcast.34), calls=%async_computation | async-start | bytes 1769472 | tf_op jit(solution)/shard_map/all_to_all | solution.py:51
  31.8 1.1 collective-permute-start.26
  32.9 3.0 collective-permute-start.21
  36.0 3.5 collective-permute-start.22
  39.4 22.1 %collective-permute-done.21 = s32[3]{0:T(128)S(1)} collective-permute-done((s32[3]{0:T(128)S(1)}, s32[3]{0:T(128)S(1)}, u32[]{:S(2)}, u32[]{:S(2)}) %collective-permute-start.21) | collective-permute-done | bytes 44 | tf_op jit(solution)/shard_map/ppermute | solution.py:40
  61.6 1.3 collective-permute-start.23
  62.9 1.3 collective-permute-start.24
  64.2 21.3 %collective-permute-done.23 = s32[3]{0:T(128)S(1)} collective-permute-done((s32[3]{0:T(128)S(1)}, s32[3]{0:T(128)S(1)}, u32[]{:S(2)}, u32[]{:S(2)}) %collective-permute-start.23) | collective-permute-done | bytes 44 | tf_op jit(solution)/shard_map/ppermute | solution.py:40
  85.4 1.3 collective-permute-start.25
  86.7 1.5 collective-permute-done.24
  88.2 4.9 %collective-permute-start.14 = (bf16[1152,384]{1,0:T(8,128)(2,1)S(1)}, bf16[1152,384]{1,0:T(8,128)(2,1)}, u32[]{:S(2)}, u32[]{:S(2)}) collective-permute-start(bf16[1152,384]{1,0:T(8,128)(2,1)S(1)} %constant_dynamic-update-slice_fusion.18), channel_id=1, source_target_pairs={{0,4},{4,8},{8,12},{1,5},{5,9},{9,13},{2,6},{6,10},{10,14},{3,7},{... | collective-permute-start | bytes 2654216 | tf_op jit(solution)/shard_map/ppermute | solution.py:40
  93.7 1.4 collective-permute-start
  95.1 1.9 concatenate.11
  97.0 1.3 collective-permute-start.15
  98.3 1.7 constant_dynamic-update-slice_fusion.17
  100.0 1.3 collective-permute-start.16
  101.3 1.7 constant_dynamic-update-slice_fusion.8
  103.0 1.3 collective-permute-start.17
  104.3 1.1 constant_dynamic-update-slice_fusion.16
  106.2 1.1 constant_dynamic-update-slice_fusion.15
  107.2 2.9 collective-permute-done.14
  110.1 5.4 %collective-permute-start.1 = (bf16[1152,384]{1,0:T(8,128)(2,1)S(1)}, bf16[1152,384]{1,0:T(8,128)(2,1)S(1)}, u32[]{:S(2)}, u32[]{:S(2)}) collective-permute-start(bf16[1152,384]{1,0:T(8,128)(2,1)S(1)} %bitcast.52), channel_id=1, source_target_pairs={{0,12},{1,13},{2,14},{3,15},{16,28},{17,29},{18,30},{19,31}} | collective-permute-start | bytes 2654216 | tf_op jit(solution)/shard_map/ppermute | solution.py:40
  115.6 2.2 constant_dynamic-update-slice_fusion.14
  118.7 1.7 collective-permute-done.15
  120.4 38.9 %collective-permute-start.2 = (bf16[1152,384]{1,0:T(8,128)(2,1)S(1)}, bf16[1152,384]{1,0:T(8,128)(2,1)S(1)}, u32[]{:S(2)}, u32[]{:S(2)}) collective-permute-start(bf16[1152,384]{1,0:T(8,128)(2,1)S(1)} %bitcast.53), channel_id=1, source_target_pairs={{0,8},{4,12},{1,9},{5,13},{2,10},{6,14},{3,11},{7,15},{16,24},{20,... | collective-permute-start | bytes 2654216 | tf_op jit(solution)/shard_map/ppermute | solution.py:40
  160.3 14.4 %collective-permute-done.16 = bf16[1152,384]{1,0:T(8,128)(2,1)S(1)} collective-permute-done((bf16[1152,384]{1,0:T(8,128)(2,1)S(1)}, bf16[1152,384]{1,0:T(8,128)(2,1)S(1)}, u32[]{:S(2)}, u32[]{:S(2)}) %collective-permute-start.16) | collective-permute-done | bytes 884768 | tf_op jit(solution)/shard_map/ppermute | solution.py:40
  174.7 1.3 collective-permute-start.3
  177.1 1.3 collective-permute-start.4
  179.4 1.3 collective-permute-start.5
  181.5 1.3 collective-permute-start.6
  185.5 7.9 %collective-permute-done.3 = bf16[1152,384]{1,0:T(8,128)(2,1)S(1)} collective-permute-done((bf16[1152,384]{1,0:T(8,128)(2,1)S(1)}, bf16[1152,384]{1,0:T(8,128)(2,1)S(1)}, u32[]{:S(2)}, u32[]{:S(2)}) %collective-permute-start.3) | collective-permute-done | bytes 884768 | tf_op jit(solution)/shard_map/ppermute | solution.py:40
  195.4 4.3 %collective-permute-done.4 = bf16[1152,384]{1,0:T(8,128)(2,1)S(1)} collective-permute-done((bf16[1152,384]{1,0:T(8,128)(2,1)S(1)}, bf16[1152,384]{1,0:T(8,128)(2,1)S(1)}, u32[]{:S(2)}, u32[]{:S(2)}) %collective-permute-start.4) | collective-permute-done | bytes 884768 | tf_op jit(solution)/shard_map/ppermute | solution.py:40
  200.7 54.6 %collective-permute-done.5 = bf16[1152,384]{1,0:T(8,128)(2,1)S(1)} collective-permute-done((bf16[1152,384]{1,0:T(8,128)(2,1)S(1)}, bf16[1152,384]{1,0:T(8,128)(2,1)S(1)}, u32[]{:S(2)}, u32[]{:S(2)}) %collective-permute-start.5) | collective-permute-done | bytes 884768 | tf_op jit(solution)/shard_map/ppermute | solution.py:40
  255.3 1.1 constant_dynamic-update-slice_fusion.2
  258.1 76.2 %while.27 = (s32[]{:T(128)}, bf16[3,384,384]{2,1,0:T(8,128)(2,1)}, s32[3]{0:T(128)S(1)}, bf16[3,384,384]{2,1,0:T(8,128)(2,1)}, s32[3,8]{1,0:T(4,128)S(1)}, /*ind...) while((s32[]{:T(128)}, bf16[3,384,384]{2,1,0:T(8,128)(2,1)}, ...), condition=%wide.region_5.6_spmd.clone, body=%wide.region_0.5_spmd.clone.sunk | while | flops 612344704 | bytes 26889600 | solution.py:110
  261.3 4.0 %gather_fusion.1 = bf16[8,384,384]{2,1,0:T(8,128)(2,1)S(1)} fusion(bf16[23,384,384]{2,1,0:T(8,128)(2,1)} %get-tuple-element.426, s32[1024]{0:T(1024)S(1)} %pad_clamp_fusion.2), kind=kCustom, calls=%fused_computation.1.clone.clone.1 | custom fusion | bytes 4718624 | tf_op jit(solution)/shard_map/while/body/eval_jaxpr/gather | solution.py:86
  265.3 5.2 %gather_fusion.2 = bf16[8,384,384]{2,1,0:T(8,128)(2,1)} fusion(bf16[23,384,384]{2,1,0:T(8,128)(2,1)} %get-tuple-element.427, s32[1024]{0:T(1024)S(1)} %pad_clamp_fusion.2), kind=kCustom, calls=%fused_computation.2.clone.clone.1 | custom fusion | bytes 4718624 | tf_op jit(solution)/shard_map/while/body/eval_jaxpr/gather | solution.py:87
  271.5 11.2 %while.28 = (s32[]{:T(128)}, bf16[384,384]{1,0:T(8,128)(2,1)S(1)}, pred[8,384]{1,0:T(8,128)(4,1)}, bf16[384,384]{1,0:T(8,128)(2,1)S(1)}, bf16[3072,384]{1,0:T(8,...) while((s32[]{:T(128)}, bf16[384,384]{1,0:T(8,128)(2,1)S(1)}, ...), condition=%wide.wide.region_4.4_spmd, body=%wide.wide.region_1.3_spmd.sunk | while | flops 612334848 | bytes 15939227 | solution.py:108
  273.2 2.0 fusion.43
  277.0 2.0 fusion.43
  280.7 2.0 fusion.43
  286.7 4.0 %gather_fusion.1 = bf16[8,384,384]{2,1,0:T(8,128)(2,1)S(1)} fusion(bf16[23,384,384]{2,1,0:T(8,128)(2,1)} %get-tuple-element.426, s32[1024]{0:T(1024)S(1)} %pad_clamp_fusion.2), kind=kCustom, calls=%fused_computation.1.clone.clone.1 | custom fusion | bytes 4718624 | tf_op jit(solution)/shard_map/while/body/eval_jaxpr/gather | solution.py:86
  290.7 5.2 %gather_fusion.2 = bf16[8,384,384]{2,1,0:T(8,128)(2,1)} fusion(bf16[23,384,384]{2,1,0:T(8,128)(2,1)} %get-tuple-element.427, s32[1024]{0:T(1024)S(1)} %pad_clamp_fusion.2), kind=kCustom, calls=%fused_computation.2.clone.clone.1 | custom fusion | bytes 4718624 | tf_op jit(solution)/shard_map/while/body/eval_jaxpr/gather | solution.py:87
  296.9 11.2 %while.28 = (s32[]{:T(128)}, bf16[384,384]{1,0:T(8,128)(2,1)S(1)}, pred[8,384]{1,0:T(8,128)(4,1)}, bf16[384,384]{1,0:T(8,128)(2,1)S(1)}, bf16[3072,384]{1,0:T(8,...) while((s32[]{:T(128)}, bf16[384,384]{1,0:T(8,128)(2,1)S(1)}, ...), condition=%wide.wide.region_4.4_spmd, body=%wide.wide.region_1.3_spmd.sunk | while | flops 612334848 | bytes 15939227 | solution.py:108
  298.6 2.0 fusion.43
  302.3 2.0 fusion.43
  306.1 2.0 fusion.43
  312.0 4.0 %gather_fusion.1 = bf16[8,384,384]{2,1,0:T(8,128)(2,1)S(1)} fusion(bf16[23,384,384]{2,1,0:T(8,128)(2,1)} %get-tuple-element.426, s32[1024]{0:T(1024)S(1)} %pad_clamp_fusion.2), kind=kCustom, calls=%fused_computation.1.clone.clone.1 | custom fusion | bytes 4718624 | tf_op jit(solution)/shard_map/while/body/eval_jaxpr/gather | solution.py:86
  316.0 5.2 %gather_fusion.2 = bf16[8,384,384]{2,1,0:T(8,128)(2,1)} fusion(bf16[23,384,384]{2,1,0:T(8,128)(2,1)} %get-tuple-element.427, s32[1024]{0:T(1024)S(1)} %pad_clamp_fusion.2), kind=kCustom, calls=%fused_computation.2.clone.clone.1 | custom fusion | bytes 4718624 | tf_op jit(solution)/shard_map/while/body/eval_jaxpr/gather | solution.py:87
  322.3 11.2 %while.28 = (s32[]{:T(128)}, bf16[384,384]{1,0:T(8,128)(2,1)S(1)}, pred[8,384]{1,0:T(8,128)(4,1)}, bf16[384,384]{1,0:T(8,128)(2,1)S(1)}, bf16[3072,384]{1,0:T(8,...) while((s32[]{:T(128)}, bf16[384,384]{1,0:T(8,128)(2,1)S(1)}, ...), condition=%wide.wide.region_4.4_spmd, body=%wide.wide.region_1.3_spmd.sunk | while | flops 612334848 | bytes 15939227 | solution.py:108
  324.0 2.0 fusion.43
  327.7 2.0 fusion.43
  331.5 2.0 fusion.43
  334.3 16.1 %all_to_all.54 = bf16[4,288,384]{2,1,0:T(8,128)(2,1)S(1)} all-to-all(bf16[4,288,384]{2,1,0:T(8,128)(2,1)} %bitcast.62), channel_id=1, replica_groups=mesh['clips'=2,'ctx'=4,'head'=4] {'head'}, dimensions={0} | all-to-all | bytes 1769472 | tf_op jit(solution)/shard_map/all_to_all | solution.py:112
  (116 shorter events, 44.6 us)
Async XLA Ops:
  0.0 32.9 %copy-start.3 = (s32[3]{0:T(128)S(1)}, s32[3]{0:T(128)}, u32[]{:S(2)}) copy-start(s32[3]{0:T(128)} %param.13) | copy-start | bytes 40
  0.0 18.6 %copy-start = (bf16[288,1536]{1,0:T(8,128)(2,1)S(1)}, bf16[288,1536]{1,0:T(8,128)(2,1)}, u32[]{:S(2)}) copy-start(bf16[288,1536]{1,0:T(8,128)(2,1)} %param.9) | copy-start | bytes 2654212
  0.0 95.0 %copy-start.4 = (s32[3,8]{1,0:T(4,128)S(1)}, s32[3,8]{1,0:T(4,128)}, u32[]{:S(2)}) copy-start(s32[3,8]{1,0:T(4,128)} %param.12) | copy-start | bytes 292
  1.5 18.1 %collective-permute-start.8 = (bf16[288,384]{1,0:T(8,128)(2,1)S(1)}, bf16[288,384]{1,0:T(8,128)(2,1)}, u32[]{:S(2)}, u32[]{:S(2)}) collective-permute-start(bf16[288,384]{1,0:T(8,128)(2,1)S(1)} %get-tuple-element.210), channel_id=1, source_target_pairs={{0,1},{1,0},{2,3},{3,2},{4,5},{5,4},{6,7},{7,6},{8,9},{9,8},{10,11... | collective-permute-start | bytes 663560 | tf_op jit(solution)/shard_map/ppermute | solution.py:30
  2.1 18.5 %collective-permute-start.9 = (bf16[288,384]{1,0:T(8,128)(2,1)S(1)}, bf16[288,384]{1,0:T(8,128)(2,1)}, u32[]{:S(2)}, u32[]{:S(2)}) collective-permute-start(bf16[288,384]{1,0:T(8,128)(2,1)S(1)} %get-tuple-element.212), channel_id=1, source_target_pairs={{0,2},{1,3},{2,0},{3,1},{4,6},{5,7},{6,4},{7,5},{8,10},{9,11},{10,... | collective-permute-start | bytes 663560 | tf_op jit(solution)/shard_map/ppermute | solution.py:30
  4.7 16.9 %collective-permute-start.10 = (bf16[288,384]{1,0:T(8,128)(2,1)S(1)}, bf16[288,384]{1,0:T(8,128)(2,1)S(1)}, u32[]{:S(2)}, u32[]{:S(2)}) collective-permute-start(bf16[288,384]{1,0:T(8,128)(2,1)S(1)} %get-tuple-element.209), channel_id=1, source_target_pairs={{0,3},{1,2},{2,1},{3,0},{4,7},{5,6},{6,5},{7,4},{8,11},{9,10},{10,... | collective-permute-start | bytes 663560 | tf_op jit(solution)/shard_map/ppermute | solution.py:30
  6.9 19.7 %all-to-all-start.1 = ((bf16[288,4,384]{2,0,1:T(8,128)(2,1)}), bf16[288,4,384]{2,0,1:T(8,128)(2,1)S(1)}, u32[]{:S(2)}, u32[]{:S(2)}) async-start(bf16[288,4,384]{2,0,1:T(8,128)(2,1)} %bitcast.33), calls=%async_computation.1 | async-start | bytes 1769472 | tf_op jit(solution)/shard_map/all_to_all | solution.py:52
  10.4 25.5 %collective-permute-start.20 = (s32[3]{0:T(128)}, s32[3]{0:T(128)S(1)}, u32[]{:S(2)}, u32[]{:S(2)}) collective-permute-start(s32[3]{0:T(128)} %param.13), channel_id=1, source_target_pairs={{0,12},{1,13},{2,14},{3,15},{16,28},{17,29},{18,30},{19,31}} | collective-permute-start | bytes 44 | tf_op jit(solution)/shard_map/ppermute | solution.py:40
  17.5 14.3 %collective-permute-start.19 = (s32[1]{0:T(128)}, s32[1]{0:T(128)}, u32[]{:S(2)}, u32[]{:S(2)}) collective-permute-start(s32[1]{0:T(128)} %get-tuple-element.216), channel_id=1, source_target_pairs={} | collective-permute-start | bytes 20 | tf_op jit(solution)/shard_map/ppermute | solution.py:40
  21.7 81.3 %collective-permute-start.12 = (bf16[1152,384]{1,0:T(8,128)(2,1)S(1)}, bf16[1152,384]{1,0:T(8,128)(2,1)S(1)}, u32[]{:S(2)}, u32[]{:S(2)}) collective-permute-start(bf16[1152,384]{1,0:T(8,128)(2,1)S(1)} %constant_dynamic-update-slice_fusion.18), channel_id=1, source_target_pairs={{0,12},{1,13},{2,14},{3,15},{16,28},{17,29},{18,30},{19,31}} | collective-permute-start | bytes 2654216 | tf_op jit(solution)/shard_map/ppermute | solution.py:40
  23.1 82.3 %collective-permute-start.13 = (bf16[1152,384]{1,0:T(8,128)(2,1)S(1)}, bf16[1152,384]{1,0:T(8,128)(2,1)S(1)}, u32[]{:S(2)}, u32[]{:S(2)}) collective-permute-start(bf16[1152,384]{1,0:T(8,128)(2,1)S(1)} %constant_dynamic-update-slice_fusion.18), channel_id=1, source_target_pairs={{0,8},{4,12},{1,9},{5,13},{2,10},{6,14},{3,11},{7,15},{16,24},{20,... | collective-permute-start | bytes 2654216 | tf_op jit(solution)/shard_map/ppermute | solution.py:40
  25.3 71.7 %collective-permute-start.11 = (bf16[384,384]{1,0:T(8,128)(2,1)}, bf16[384,384]{1,0:T(8,128)(2,1)}, u32[]{:S(2)}, u32[]{:S(2)}) collective-permute-start(bf16[384,384]{1,0:T(8,128)(2,1)} %get-tuple-element.208), channel_id=1, source_target_pairs={} | collective-permute-start | bytes 884744 | tf_op jit(solution)/shard_map/ppermute | solution.py:40
  26.6 231.5 %all-to-all-start = ((bf16[288,4,384]{2,0,1:T(8,128)(2,1)}), bf16[288,4,384]{2,0,1:T(8,128)(2,1)}, u32[]{:S(2)}, u32[]{:S(2)}) async-start(bf16[288,4,384]{2,0,1:T(8,128)(2,1)} %bitcast.34), calls=%async_computation | async-start | bytes 1769472 | tf_op jit(solution)/shard_map/all_to_all | solution.py:51
  31.8 1.1 collective-permute-start.26
  32.9 28.7 %collective-permute-start.21 = (s32[3]{0:T(128)S(1)}, s32[3]{0:T(128)S(1)}, u32[]{:S(2)}, u32[]{:S(2)}) collective-permute-start(s32[3]{0:T(128)S(1)} %copy-done.3), channel_id=1, source_target_pairs={{0,8},{4,12},{1,9},{5,13},{2,10},{6,14},{3,11},{7,15},{16,24},{20,... | collective-permute-start | bytes 44 | tf_op jit(solution)/shard_map/ppermute | solution.py:40
  36.0 26.9 %collective-permute-start.22 = (s32[3]{0:T(128)S(1)}, s32[3]{0:T(128)S(1)}, u32[]{:S(2)}, u32[]{:S(2)}) collective-permute-start(s32[3]{0:T(128)S(1)} %copy-done.3), channel_id=1, source_target_pairs={{0,4},{4,8},{8,12},{1,5},{5,9},{9,13},{2,6},{6,10},{10,14},{3,7},{... | collective-permute-start | bytes 44 | tf_op jit(solution)/shard_map/ppermute | solution.py:40
  61.6 31.6 %copy-start.5 = (s32[3]{0:T(128)}, s32[3]{0:T(128)S(1)}, u32[]{:S(2)}) copy-start(s32[3]{0:T(128)S(1)} %collective-permute-done.21) | copy-start | bytes 40
  61.6 23.9 %collective-permute-start.23 = (s32[3]{0:T(128)S(1)}, s32[3]{0:T(128)S(1)}, u32[]{:S(2)}, u32[]{:S(2)}) collective-permute-start(s32[3]{0:T(128)S(1)} %copy-done.3), channel_id=1, source_target_pairs={{4,0},{8,4},{12,8},{5,1},{9,5},{13,9},{6,2},{10,6},{14,10},{7,3},{... | collective-permute-start | bytes 44 | tf_op jit(solution)/shard_map/ppermute | solution.py:40
  62.9 30.3 %copy-start.6 = (s32[3]{0:T(128)}, s32[3]{0:T(128)S(1)}, u32[]{:S(2)}) copy-start(s32[3]{0:T(128)S(1)} %collective-permute-done.22) | copy-start | bytes 40
  62.9 25.3 %collective-permute-start.24 = (s32[3]{0:T(128)S(1)}, s32[3]{0:T(128)S(1)}, u32[]{:S(2)}, u32[]{:S(2)}) collective-permute-start(s32[3]{0:T(128)S(1)} %copy-done.3), channel_id=1, source_target_pairs={{8,0},{12,4},{9,1},{13,5},{10,2},{14,6},{11,3},{15,7},{24,16},{28,... | collective-permute-start | bytes 44 | tf_op jit(solution)/shard_map/ppermute | solution.py:40
  85.4 7.7 %copy-start.7 = (s32[3]{0:T(128)}, s32[3]{0:T(128)S(1)}, u32[]{:S(2)}) copy-start(s32[3]{0:T(128)S(1)} %collective-permute-done.23) | copy-start | bytes 40
  85.4 7.7 %collective-permute-start.25 = (s32[3]{0:T(128)S(1)}, s32[3]{0:T(128)S(1)}, u32[]{:S(2)}, u32[]{:S(2)}) collective-permute-start(s32[3]{0:T(128)S(1)} %copy-done.3), channel_id=1, source_target_pairs={{12,0},{13,1},{14,2},{15,3},{28,16},{29,17},{30,18},{31,19}} | collective-permute-start | bytes 44 | tf_op jit(solution)/shard_map/ppermute | solution.py:40
  88.2 5.0 %copy-start.8 = (s32[3]{0:T(128)}, s32[3]{0:T(128)S(1)}, u32[]{:S(2)}) copy-start(s32[3]{0:T(128)S(1)} %collective-permute-done.24) | copy-start | bytes 40
  88.2 21.9 %collective-permute-start.14 = (bf16[1152,384]{1,0:T(8,128)(2,1)S(1)}, bf16[1152,384]{1,0:T(8,128)(2,1)}, u32[]{:S(2)}, u32[]{:S(2)}) collective-permute-start(bf16[1152,384]{1,0:T(8,128)(2,1)S(1)} %constant_dynamic-update-slice_fusion.18), channel_id=1, source_target_pairs={{0,4},{4,8},{8,12},{1,5},{5,9},{9,13},{2,6},{6,10},{10,14},{3,7},{... | collective-permute-start | bytes 2654216 | tf_op jit(solution)/shard_map/ppermute | solution.py:40
  93.1 0.5 copy-start.9
  93.7 6.3 %collective-permute-start = (bf16[384,384]{1,0:T(8,128)(2,1)}, bf16[384,384]{1,0:T(8,128)(2,1)}, u32[]{:S(2)}, u32[]{:S(2)}) collective-permute-start(bf16[384,384]{1,0:T(8,128)(2,1)} %get-tuple-element.214), channel_id=1, source_target_pairs={} | collective-permute-start | bytes 884744 | tf_op jit(solution)/shard_map/ppermute | solution.py:40
  97.0 23.4 %collective-permute-start.15 = (bf16[1152,384]{1,0:T(8,128)(2,1)S(1)}, bf16[1152,384]{1,0:T(8,128)(2,1)S(1)}, u32[]{:S(2)}, u32[]{:S(2)}) collective-permute-start(bf16[1152,384]{1,0:T(8,128)(2,1)S(1)} %constant_dynamic-update-slice_fusion.18), channel_id=1, source_target_pairs={{4,0},{8,4},{12,8},{5,1},{9,5},{13,9},{6,2},{10,6},{14,10},{7,3},{... | collective-permute-start | bytes 2654216 | tf_op jit(solution)/shard_map/ppermute | solution.py:40
  100.0 74.7 %collective-permute-start.16 = (bf16[1152,384]{1,0:T(8,128)(2,1)S(1)}, bf16[1152,384]{1,0:T(8,128)(2,1)S(1)}, u32[]{:S(2)}, u32[]{:S(2)}) collective-permute-start(bf16[1152,384]{1,0:T(8,128)(2,1)S(1)} %constant_dynamic-update-slice_fusion.18), channel_id=1, source_target_pairs={{8,0},{12,4},{9,1},{13,5},{10,2},{14,6},{11,3},{15,7},{24,16},{28,... | collective-permute-start | bytes 2654216 | tf_op jit(solution)/shard_map/ppermute | solution.py:40
  103.0 74.1 %collective-permute-start.17 = (bf16[1152,384]{1,0:T(8,128)(2,1)S(1)}, bf16[1152,384]{1,0:T(8,128)(2,1)S(1)}, u32[]{:S(2)}, u32[]{:S(2)}) collective-permute-start(bf16[1152,384]{1,0:T(8,128)(2,1)S(1)} %constant_dynamic-update-slice_fusion.18), channel_id=1, source_target_pairs={{12,0},{13,1},{14,2},{15,3},{28,16},{29,17},{30,18},{31,19}} | collective-permute-start | bytes 2654216 | tf_op jit(solution)/shard_map/ppermute | solution.py:40
  105.3 78.4 %copy-start.2 = (bf16[384,384]{1,0:T(8,128)(2,1)S(1)}, bf16[384,384]{1,0:T(8,128)(2,1)}, u32[]{:S(2)}) copy-start(bf16[384,384]{1,0:T(8,128)(2,1)} %get-tuple-element.213) | copy-start | bytes 884740
  105.4 74.1 %collective-permute-start.18 = (bf16[384,384]{1,0:T(8,128)(2,1)}, bf16[384,384]{1,0:T(8,128)(2,1)S(1)}, u32[]{:S(2)}, u32[]{:S(2)}) collective-permute-start(bf16[384,384]{1,0:T(8,128)(2,1)} %get-tuple-element.207), channel_id=1, source_target_pairs={} | collective-permute-start | bytes 884744 | tf_op jit(solution)/shard_map/ppermute | solution.py:40
  110.1 71.3 %collective-permute-start.1 = (bf16[1152,384]{1,0:T(8,128)(2,1)S(1)}, bf16[1152,384]{1,0:T(8,128)(2,1)S(1)}, u32[]{:S(2)}, u32[]{:S(2)}) collective-permute-start(bf16[1152,384]{1,0:T(8,128)(2,1)S(1)} %bitcast.52), channel_id=1, source_target_pairs={{0,12},{1,13},{2,14},{3,15},{16,28},{17,29},{18,30},{19,31}} | collective-permute-start | bytes 2654216 | tf_op jit(solution)/shard_map/ppermute | solution.py:40
  120.4 63.4 %collective-permute-start.2 = (bf16[1152,384]{1,0:T(8,128)(2,1)S(1)}, bf16[1152,384]{1,0:T(8,128)(2,1)S(1)}, u32[]{:S(2)}, u32[]{:S(2)}) collective-permute-start(bf16[1152,384]{1,0:T(8,128)(2,1)S(1)} %bitcast.53), channel_id=1, source_target_pairs={{0,8},{4,12},{1,9},{5,13},{2,10},{6,14},{3,11},{7,15},{16,24},{20,... | collective-permute-start | bytes 2654216 | tf_op jit(solution)/shard_map/ppermute | solution.py:40
  174.7 18.6 %collective-permute-start.3 = (bf16[1152,384]{1,0:T(8,128)(2,1)S(1)}, bf16[1152,384]{1,0:T(8,128)(2,1)S(1)}, u32[]{:S(2)}, u32[]{:S(2)}) collective-permute-start(bf16[1152,384]{1,0:T(8,128)(2,1)S(1)} %bitcast.54), channel_id=1, source_target_pairs={{0,4},{4,8},{8,12},{1,5},{5,9},{9,13},{2,6},{6,10},{10,14},{3,7},{... | collective-permute-start | bytes 2654216 | tf_op jit(solution)/shard_map/ppermute | solution.py:40
  177.1 22.6 %collective-permute-start.4 = (bf16[1152,384]{1,0:T(8,128)(2,1)S(1)}, bf16[1152,384]{1,0:T(8,128)(2,1)S(1)}, u32[]{:S(2)}, u32[]{:S(2)}) collective-permute-start(bf16[1152,384]{1,0:T(8,128)(2,1)S(1)} %bitcast.55), channel_id=1, source_target_pairs={{4,0},{8,4},{12,8},{5,1},{9,5},{13,9},{6,2},{10,6},{14,10},{7,3},{... | collective-permute-start | bytes 2654216 | tf_op jit(solution)/shard_map/ppermute | solution.py:40
  179.4 75.8 %collective-permute-start.5 = (bf16[1152,384]{1,0:T(8,128)(2,1)S(1)}, bf16[1152,384]{1,0:T(8,128)(2,1)S(1)}, u32[]{:S(2)}, u32[]{:S(2)}) collective-permute-start(bf16[1152,384]{1,0:T(8,128)(2,1)S(1)} %bitcast.56), channel_id=1, source_target_pairs={{8,0},{12,4},{9,1},{13,5},{10,2},{14,6},{11,3},{15,7},{24,16},{28,... | collective-permute-start | bytes 2654216 | tf_op jit(solution)/shard_map/ppermute | solution.py:40
  181.5 74.8 %collective-permute-start.6 = (bf16[1152,384]{1,0:T(8,128)(2,1)S(1)}, bf16[1152,384]{1,0:T(8,128)(2,1)S(1)}, u32[]{:S(2)}, u32[]{:S(2)}) collective-permute-start(bf16[1152,384]{1,0:T(8,128)(2,1)S(1)} %bitcast.57), channel_id=1, source_target_pairs={{12,0},{13,1},{14,2},{15,3},{28,16},{29,17},{30,18},{31,19}} | collective-permute-start | bytes 2654216 | tf_op jit(solution)/shard_map/ppermute | solution.py:40
  183.8 73.5 %collective-permute-start.7 = (bf16[384,384]{1,0:T(8,128)(2,1)S(1)}, bf16[384,384]{1,0:T(8,128)(2,1)S(1)}, u32[]{:S(2)}, u32[]{:S(2)}) collective-permute-start(bf16[384,384]{1,0:T(8,128)(2,1)S(1)} %copy-done.2), channel_id=1, source_target_pairs={} | collective-permute-start | bytes 884744 | tf_op jit(solution)/shard_map/ppermute | solution.py:40
  261.2 10.2 %copy-start.1 = (pred[8,384]{1,0:T(8,128)(4,1)}, pred[8,384]{1,0:T(8,128)(4,1)S(1)}, u32[]{:S(2)}) copy-start(pred[8,384]{1,0:T(8,128)(4,1)S(1)} %gather_fusion) | copy-start | bytes 9220 | tf_op jit(solution)/shard_map/while
  286.6 10.2 %copy-start.1 = (pred[8,384]{1,0:T(8,128)(4,1)}, pred[8,384]{1,0:T(8,128)(4,1)S(1)}, u32[]{:S(2)}) copy-start(pred[8,384]{1,0:T(8,128)(4,1)S(1)} %gather_fusion) | copy-start | bytes 9220 | tf_op jit(solution)/shard_map/while
  312.0 10.2 %copy-start.1 = (pred[8,384]{1,0:T(8,128)(4,1)}, pred[8,384]{1,0:T(8,128)(4,1)S(1)}, u32[]{:S(2)}) copy-start(pred[8,384]{1,0:T(8,128)(4,1)S(1)} %gather_fusion) | copy-start | bytes 9220 | tf_op jit(solution)/shard_map/while
